TPU v7x, 32 devices: a whole 2x2x4 slice. The times are simulated.
32 devices in a mesh: paths: 2 (over x), qa: 8 (over z, y), qb: 2 (over core).
Axes of the slice: x: 2, y: 2, z: 4, core: 2. Of those that a mesh axis runs over, the one named last changes fastest.
Arguments:
- state: float32 [2, 4194304], P(None, ('paths', 'qa', 'qb')), parts along dimension 1, may hold values from -6 to 6
- gate_terms: float32 [18, 2, 2, 128, 128], replicated, may hold values from -0.375 to 0.375
- path_bits: int32 [36], P('paths'), parts along dimension 0, may hold values from 0 to 1
Outputs:
- final_state: float32 [2, 4194304], P(None, ('paths', 'qa', 'qb')), parts along dimension 1
There are 2 independent parts, one for each index of `paths`. A program takes and returns all parts, laid end to end along the dimension named above; an argument that names none is the same for every part. Nothing has to cross between parts.
All inputs are finite; a program needn't handle non-finite values.
Results may differ from a plain program's by a relative error of at most 0.00013.
Values sent between devices are 32-bit elements; how exact they have to be, the bound alone decides.
A program may use at most 64 MiB of HBM per device.

v0:
```python
import functools

import jax
import jax.numpy as jnp
from jax import lax
from jax.experimental import pallas as pl
from jax.experimental.pallas import tpu as pltpu
from jax.sharding import PartitionSpec as P

MESH = pl.DeviceIdType.MESH
HIGHEST = lax.Precision.HIGHEST


def window_offsets(span, gate_bits):
    return [0, span, gate_bits, span - 1, gate_bits + 1, span - 2]


def row_gates(local_bits, gate_bits):
    sections = []
    for section, drop in enumerate((0, 1, 0)):
        merged = []
        for index, offset in enumerate(window_offsets(local_bits - gate_bits - drop, gate_bits)):
            if offset == 0:
                continue
            gate = 6 * section + index
            if merged and merged[-1][0] == offset - gate_bits:
                merged[-1][1].append(gate)
            else:
                merged.append((offset - gate_bits, [gate]))
        sections.append(merged)
    return sections


def split(x):
    high = x.astype(jnp.bfloat16)
    return high, (x - high.astype(jnp.float32)).astype(jnp.bfloat16)


def kernel(n_qa, sections, x_hbm, terms_hbm, bits_ref, out_ref,
           first, other, second, terms, weights, lane_weights,
           send_one, recv_one, send_two, recv_two, local_sem):
    qa = lax.axis_index("qa")
    qb = lax.axis_index("qb")
    rows, dim = x_hbm.shape
    block = rows // n_qa
    half = rows // 2
    low = rows // 4 // n_qa // (n_qa // 2) * 2
    middle = half // (n_qa * low)

    fetch = pltpu.make_async_copy(terms_hbm, terms, local_sem.at[0])
    fetch.start()

    barrier = pltpu.get_barrier_semaphore()
    for d in range(n_qa):
        for b in range(2):
            if d or b:
                pl.semaphore_signal(
                    barrier, inc=1,
                    device_id={"qa": lax.rem(qa + d, n_qa), "qb": lax.rem(qb + b, 2)},
                    device_id_type=MESH,
                )
    pl.semaphore_wait(barrier, 2 * n_qa - 1)

    def rows_of(which):
        return pl.ds(pl.multiple_of(which * block, block), block)

    def copy_one(d):
        peer = lax.rem(qa + d, n_qa)
        return pltpu.make_async_remote_copy(
            src_ref=x_hbm.at[rows_of(peer)],
            dst_ref=first.at[rows_of(qa)],
            send_sem=send_one.at[d],
            recv_sem=recv_one.at[d],
            device_id={"qa": peer},
            device_id_type=MESH,
        )

    ones = [copy_one(d) for d in range(1, n_qa)]
    for copy in ones:
        copy.start()
    own = pltpu.make_async_copy(x_hbm.at[rows_of(qa)], first.at[rows_of(qa)], local_sem.at[1])
    own.start()

    fetch.wait()

    def blocked(re, im):
        return jnp.concatenate(
            [jnp.concatenate([re, -im], axis=1), jnp.concatenate([im, re], axis=1)], axis=0
        )

    def product(gates):
        re = terms[gates[0], bits_ref[gates[0]], 0]
        im = terms[gates[0], bits_ref[gates[0]], 1]
        for gate in gates[1:]:
            left = blocked(terms[gate, bits_ref[gate], 0], terms[gate, bits_ref[gate], 1])
            both = jnp.dot(
                left, jnp.concatenate([re, im], axis=0),
                preferred_element_type=jnp.float32, precision=HIGHEST,
            )
            re, im = both[:dim], both[dim:]
        return blocked(re, im)

    lane_high, lane_low = split(product([0, 6, 12]))
    lane_weights[0] = lane_high
    lane_weights[1] = lane_low
    slot = 0
    for section in sections:
        for _, gates in section:
            high, lower = split(product(gates))
            weights[slot, : 2 * dim] = high
            weights[slot, 2 * dim :] = lower
            slot += 1

    def lanes(which):
        base = which * block
        count = block // 2
        re = first[pl.ds(base, count, stride=2), :]
        im = first[pl.ds(base + 1, count, stride=2), :]
        high, lower = split(jnp.concatenate([re, im], axis=1))
        dims = (((1,), (1,)), ((), ()))
        dot = functools.partial(
            lax.dot_general, dimension_numbers=dims, preferred_element_type=jnp.float32
        )
        y = dot(high, lane_weights[0]) + (dot(lower, lane_weights[0]) + dot(high, lane_weights[1]))
        first[pl.ds(base, count, stride=2), :] = y[:, :dim]
        first[pl.ds(base + 1, count, stride=2), :] = y[:, dim:]

    own.wait()
    lanes(qa)
    for d in range(1, n_qa):
        ones[d - 1].wait_recv()
        lanes(lax.rem(qa + n_qa - d, n_qa))

    def apply(src, dst, slot, offset, base, count):
        stride = 2 ** (offset + 1)
        starts = [
            hi * stride * dim + 2 * lo for hi in range(count // (stride * dim)) for lo in range(2**offset)
        ]
        for pair in range(0, len(starts), 2):
            columns = []
            for start in starts[pair : pair + 2]:
                columns.append(jnp.concatenate([
                    src[pl.ds(base + start, dim, stride=stride), :],
                    src[pl.ds(base + start + 1, dim, stride=stride), :],
                ], axis=0))
            high, lower = split(jnp.concatenate(columns, axis=1))
            both = jnp.dot(weights[slot], high, preferred_element_type=jnp.float32)
            y = both[: 2 * dim] + (
                both[2 * dim :]
                + jnp.dot(weights[slot, : 2 * dim], lower, preferred_element_type=jnp.float32)
            )
            for j, start in enumerate(starts[pair : pair + 2]):
                dst[pl.ds(base + start, dim, stride=stride), :] = y[:dim, j * dim : (j + 1) * dim]
                dst[pl.ds(base + start + 1, dim, stride=stride), :] = y[dim:, j * dim : (j + 1) * dim]

    (s0, s1, s2, s3), (t0, t1, t2, t3), (u0, u1, u2, u3) = [[o for o, _ in s] for s in sections]
    apply(first, other, 0, s0, 0, rows)
    apply(other, first, 1, s1, 0, rows)

    def view(ref, b, k):
        return ref.reshape(2, middle, n_qa, low, dim).at[b, :, k]

    def copy_two(d, b):
        peer = lax.rem(qa + d, n_qa)
        to = lax.rem(qb + b, 2)
        return pltpu.make_async_remote_copy(
            src_ref=view(first, to, peer),
            dst_ref=view(second, qb, qa),
            send_sem=send_two.at[b, d],
            recv_sem=recv_two.at[b, d],
            device_id={"qa": peer, "qb": to},
            device_id_type=MESH,
        )

    twos = {}
    for b in range(2):
        base = pl.multiple_of(lax.rem(qb + b, 2) * half, half)
        apply(first, other, 2, s2, base, half)
        apply(other, first, 3, s3, base, half)
        for d in range(n_qa):
            if d or b:
                twos[b, d] = copy_two(d, b)
            else:
                twos[b, d] = pltpu.make_async_copy(
                    view(first, qb, qa), view(second, qb, qa), local_sem.at[2]
                )
            twos[b, d].start()

    for b in range(2):
        for d in range(n_qa):
            if d or b:
                twos[b, d].wait_recv()
            else:
                twos[b, d].wait()
        base = pl.multiple_of(lax.rem(qb + b, 2) * half, half)
        apply(second, other, 4, t0, base, half)
        apply(other, second, 5, t1, base, half)
        apply(second, other, 6, t2, base, half)
        apply(other, second, 7, t3, base, half)

    apply(second, other, 8, u0, 0, rows)
    apply(other, second, 9, u1, 0, rows)
    apply(second, other, 10, u2, 0, rows)
    apply(other, out_ref, 11, u3, 0, rows)

    for copy in ones:
        copy.wait_send()
    for (b, d), copy in twos.items():
        if d or b:
            copy.wait_send()


def per_device(state, gate_terms, path_bits):
    n_qa = lax.axis_size("qa")
    dim = gate_terms.shape[-1]
    gate_bits = dim.bit_length() - 1
    amps = state.shape[1]
    local_bits = amps.bit_length() - 1
    rows = 2 * amps // dim
    sections = row_gates(local_bits, gate_bits)
    count = sum(len(s) for s in sections)
    x = state.reshape(2, rows // 2, dim).transpose(1, 0, 2).reshape(rows, dim)
    y = pl.pallas_call(
        functools.partial(kernel, n_qa, sections),
        out_shape=jax.ShapeDtypeStruct((rows, dim), jnp.float32),
        in_specs=[
            pl.BlockSpec(memory_space=pl.ANY),
            pl.BlockSpec(memory_space=pl.ANY),
            pl.BlockSpec(memory_space=pltpu.SMEM),
        ],
        out_specs=pl.BlockSpec(memory_space=pltpu.VMEM),
        scratch_shapes=[
            pltpu.VMEM((rows, dim), jnp.float32),
            pltpu.VMEM((rows, dim), jnp.float32),
            pltpu.VMEM((rows, dim), jnp.float32),
            pltpu.VMEM(gate_terms.shape, jnp.float32),
            pltpu.VMEM((count, 4 * dim, 2 * dim), jnp.bfloat16),
            pltpu.VMEM((2, 2 * dim, 2 * dim), jnp.bfloat16),
            pltpu.SemaphoreType.DMA((n_qa,)),
            pltpu.SemaphoreType.DMA((n_qa,)),
            pltpu.SemaphoreType.DMA((2, n_qa)),
            pltpu.SemaphoreType.DMA((2, n_qa)),
            pltpu.SemaphoreType.DMA((3,)),
        ],
        compiler_params=pltpu.CompilerParams(
            collective_id=0, has_side_effects=True, vmem_limit_bytes=48 * 2**20
        ),
    )(x, gate_terms, path_bits)
    return y.reshape(rows // 2, 2, dim).transpose(1, 0, 2).reshape(2, amps)


def solution(mesh):
    return jax.shard_map(
        per_device,
        mesh=mesh,
        in_specs=(P(None, ("paths", "qa", "qb")), P(), P("paths")),
        out_specs=P(None, ("paths", "qa", "qb")),
        check_vma=False,
    )
```

profile of v0, /device:TPU:29, one launch (start us, length us, event | category | flops | bytes accessed | tf_op | source)
XLA Modules:
  0.0 60.8 jit_solution(2725790748983954356)
XLA Ops:
  0.0 0.0 copy-start
  0.0 1.2 %copy-done = f32[2,131072]{1,0:T(2,128)S(1)} copy-done((f32[2,131072]{1,0:T(2,128)S(1)}, f32[2,131072]{1,0:T(2,128)}, u32[]{:S(2)}) %copy-start) | copy-done | bytes 1048600
  1.2 0.0 copy-start.1
  1.2 0.7 %copy-done.1 = s32[18]{0:T(128)S(1)} copy-done((s32[18]{0:T(128)S(1)}, s32[18]{0:T(128)}, u32[]{:S(2)}) %copy-start.1) | copy-done | bytes 96
  1.9 57.9 %shard_map.37 = f32[2048,128]{1,0:T(8,128)S(1)} custom-call(f32[2048,128]{1,0:T(8,128)S(1)} %bitcast.11, f32[18,2,2,128,128]{4,3,2,1,0:T(8,128)} %terms_hbm.1, s32[18]{0:T(128)S(1)} %copy-done.1), custom_call_target="tpu_custom_call" | custom-call | tf_op jit(solution)/shard_map/pallas_call | solution.py:223
  59.8 1.0 %copy.7 = f32[2,131072]{1,0:T(2,128)} copy(f32[2,131072]{1,0:T(2,128)S(1)} %bitcast.10) | data formatting | bytes 2097152
Async XLA Ops:
  0.0 1.2 %copy-start = (f32[2,131072]{1,0:T(2,128)S(1)}, f32[2,131072]{1,0:T(2,128)}, u32[]{:S(2)}) copy-start(f32[2,131072]{1,0:T(2,128)} %param.3) | copy-start | bytes 3145732
  1.2 0.7 %copy-start.1 = (s32[18]{0:T(128)S(1)}, s32[18]{0:T(128)}, u32[]{:S(2)}) copy-start(s32[18]{0:T(128)} %bits_ref.1) | copy-start | bytes 220
where the time goes:
time: 61 us; the launch traced here: 60.8 us
  Pallas kernels  57.9 us (95%)
  local copies, waits for them, and re-layouts  2.85 us (5%)
    pallas_call x1, Pallas kernels, per_device(): pl.pallas_call(functools.partial(kernel, n_qa, sections), out_shape=jax.S...  57.9 us
    unnamed x5, local copies, waits for them, and re-layouts  2.85 us

commit v1 on v0

v1 whole, which is shorter than its diff:
```python
import functools

import jax
import jax.numpy as jnp
from jax import lax
from jax.experimental import pallas as pl
from jax.experimental.pallas import tpu as pltpu
from jax.sharding import PartitionSpec as P

MESH = pl.DeviceIdType.MESH
HIGHEST = lax.Precision.HIGHEST


def window_offsets(span, gate_bits):
    return [0, span, gate_bits, span - 1, gate_bits + 1, span - 2]


def row_gates(local_bits, gate_bits):
    sections = []
    for section, drop in enumerate((0, 1, 0)):
        merged = []
        for index, offset in enumerate(window_offsets(local_bits - gate_bits - drop, gate_bits)):
            if offset == 0:
                continue
            gate = 6 * section + index
            if merged and merged[-1][0] == offset - gate_bits:
                merged[-1][1].append(gate)
            else:
                merged.append((offset - gate_bits, [gate]))
        sections.append(merged)
    return sections


def split(x):
    high = x.astype(jnp.bfloat16)
    return high, (x - high.astype(jnp.float32)).astype(jnp.bfloat16)


def kernel(n_qa, sections, x_ref, terms_hbm, bits_hbm, out_ref,
           sent, first, other, second, total, terms, bits_ref, weights, lane_weights,
           send_one, recv_one, send_two, recv_two, local_sem, own_sem):
    qa = lax.axis_index("qa")
    qb = lax.axis_index("qb")
    _, rows, dim = first.shape
    lane_half = dim // 2
    block = rows // n_qa
    half = rows // 2
    low = rows // n_qa**2
    middle = half // (n_qa * low)

    fetch = pltpu.make_async_copy(terms_hbm, terms, local_sem.at[0])
    fetch.start()
    fetch_bits = pltpu.make_async_copy(bits_hbm, bits_ref, local_sem.at[1])
    fetch_bits.start()

    barrier = pltpu.get_barrier_semaphore()
    for d in range(n_qa):
        for b in range(2):
            if d or b:
                pl.semaphore_signal(
                    barrier, inc=1,
                    device_id={"qa": lax.rem(qa + d, n_qa), "qb": lax.rem(qb + b, 2)},
                    device_id_type=MESH,
                )

    def rows_of(which):
        return pl.ds(pl.multiple_of(which * block, block), block)

    def shuffle(c):
        at = slice(c * lane_half, (c + 1) * lane_half)
        for k in range(n_qa):
            re = x_ref[pl.ds(2 * k * block, block, stride=2), :]
            im = x_ref[pl.ds(2 * k * block + 1, block, stride=2), :]
            sent[c, k * block : (k + 1) * block, :] = jnp.concatenate([re[:, at], im[:, at]], axis=1)

    def copy_one(c, d):
        peer = lax.rem(qa + d, n_qa)
        src = sent.at[c, rows_of(peer)]
        dst = first.at[c, rows_of(qa)]
        if d == 0:
            return pltpu.make_async_copy(src, dst, own_sem.at[0, c])
        return pltpu.make_async_remote_copy(
            src_ref=src, dst_ref=dst, send_sem=send_one.at[c, d], recv_sem=recv_one.at[c, d],
            device_id={"qa": peer}, device_id_type=MESH,
        )

    ones = {}
    for c in range(2):
        shuffle(c)
        if c == 0:
            pl.semaphore_wait(barrier, 2 * n_qa - 1)
        for d in range(n_qa):
            ones[c, d] = copy_one(c, d)
            ones[c, d].start()

    fetch_bits.wait()
    fetch.wait()

    def product(gates):
        re = terms[gates[0], bits_ref[gates[0]], 0]
        im = terms[gates[0], bits_ref[gates[0]], 1]
        for gate in gates[1:]:
            left_re = terms[gate, bits_ref[gate], 0]
            left_im = terms[gate, bits_ref[gate], 1]
            left = jnp.concatenate([
                jnp.concatenate([left_re, -left_im], axis=1),
                jnp.concatenate([left_im, left_re], axis=1),
            ], axis=0)
            both = jnp.dot(
                left, jnp.concatenate([re, im], axis=0),
                preferred_element_type=jnp.float32, precision=HIGHEST,
            )
            re, im = both[:dim], both[dim:]
        return re, im

    slot = 0
    for section in sections:
        for _, gates in section:
            re, im = product(gates)
            high, lower = split(jnp.concatenate([re, im], axis=0))
            weights[slot, : 2 * dim, :dim] = high
            weights[slot, : 2 * dim, dim:] = high
            weights[slot, 2 * dim :, :dim] = lower
            weights[slot, 2 * dim :, dim:] = jnp.zeros_like(lower)
            slot += 1
    re, im = product([0, 6, 12])
    for c in range(2):
        at = slice(c * lane_half, (c + 1) * lane_half)
        high, lower = split(jnp.concatenate([
            jnp.concatenate([re[:, at], -im[:, at]], axis=1),
            jnp.concatenate([im[:, at], re[:, at]], axis=1),
        ], axis=0))
        lane_weights[c, :, :dim] = high
        lane_weights[c, :, dim : 2 * dim] = high
        lane_weights[c, :, 2 * dim :] = lower

    sign = jnp.where(lax.broadcasted_iota(jnp.int32, (dim, dim), 1) < lane_half, -1.0, 1.0)

    def apply(src, dst, slot, offset, base, count):
        stride = 2**offset
        starts = [hi * stride * dim + lo for hi in range(count // (stride * dim)) for lo in range(stride)]
        for pair in range(0, len(starts), 2):
            at = [
                pl.ds(base + start, dim, stride=stride) if stride > 1 else pl.ds(base + start, dim)
                for start in starts[pair : pair + 2]
            ]
            high, lower = split(jnp.concatenate([src[a, :] for a in at], axis=1))
            both = jnp.dot(
                weights[slot], jnp.concatenate([high, lower], axis=0),
                preferred_element_type=jnp.float32,
            )
            both = both[: 2 * dim] + both[2 * dim :]
            for j, a in enumerate(at):
                plain = both[:dim, j * dim : (j + 1) * dim]
                turned = both[dim:, j * dim : (j + 1) * dim]
                dst[a, :] = plain + sign * pltpu.roll(turned, lane_half, axis=1)

    (s0, s1, s2, s3), (t0, t1, t2, t3), (u0, u1, u2, u3) = [[o for o, _ in s] for s in sections]

    def view(ref, c, b, k):
        return ref.reshape(2, 2, middle, n_qa, low, dim).at[c, b, :, k]

    def copy_two(c, d, b):
        peer = lax.rem(qa + d, n_qa)
        to = lax.rem(qb + b, 2)
        src = view(first, c, to, peer)
        dst = view(second, c, qb, qa)
        if d == 0 and b == 0:
            return pltpu.make_async_copy(src, dst, own_sem.at[1, c])
        return pltpu.make_async_remote_copy(
            src_ref=src, dst_ref=dst, send_sem=send_two.at[c, b, d], recv_sem=recv_two.at[c, b, d],
            device_id={"qa": peer, "qb": to}, device_id_type=MESH,
        )

    def arrive(copy, own):
        if own:
            copy.wait()
        else:
            copy.wait_recv()

    twos = {}
    for c in range(2):
        here = first.at[c]
        for d in range(n_qa):
            arrive(ones[c, d], d == 0)
        apply(here, other, 0, s0, 0, rows)
        apply(other, here, 1, s1, 0, rows)
        for b in range(2):
            base = pl.multiple_of(lax.rem(qb + b, 2) * half, half)
            apply(here, other, 2, s2, base, half)
            apply(other, here, 3, s3, base, half)
            for d in range(n_qa):
                twos[c, d, b] = copy_two(c, d, b)
                twos[c, d, b].start()

    for c in range(2):
        here = second.at[c]
        for b in range(2):
            for d in range(n_qa):
                arrive(twos[c, d, b], d == 0 and b == 0)
            base = pl.multiple_of(lax.rem(qb + b, 2) * half, half)
            apply(here, other, 4, t0, base, half)
            apply(other, here, 5, t1, base, half)
            apply(here, other, 6, t2, base, half)
            apply(other, here, 7, t3, base, half)
        apply(here, other, 8, u0, 0, rows)
        apply(other, here, 9, u1, 0, rows)
        apply(here, other, 10, u2, 0, rows)
        apply(other, here, 11, u3, 0, rows)
        dims = (((1,), (1,)), ((), ()))
        for k in range(rows // (2 * dim)):
            at = slice(2 * k * dim, 2 * (k + 1) * dim)
            high, lower = split(here[at, :])
            y = lax.dot_general(
                jnp.concatenate([high, lower], axis=1), lane_weights[c, :, : 2 * dim], dims,
                preferred_element_type=jnp.float32,
            ) + lax.dot_general(
                high, lane_weights[c, :, 2 * dim :], dims, preferred_element_type=jnp.float32
            )
            if c == 0:
                total[at, :] = y
            else:
                y = y + total[at, :]
                out_ref[pl.ds(4 * k * dim, 2 * dim, stride=2), :] = y[:, :dim]
                out_ref[pl.ds(4 * k * dim + 1, 2 * dim, stride=2), :] = y[:, dim:]

    for (c, d), copy in ones.items():
        if d:
            copy.wait_send()
    for (c, d, b), copy in twos.items():
        if d or b:
            copy.wait_send()


def per_device(state, gate_terms, path_bits):
    n_qa = lax.axis_size("qa")
    dim = gate_terms.shape[-1]
    gate_bits = dim.bit_length() - 1
    amps = state.shape[1]
    local_bits = amps.bit_length() - 1
    rows = 2 * amps // dim
    sections = row_gates(local_bits, gate_bits)
    count = sum(len(s) for s in sections)
    x = state.reshape(2, rows // 2, dim).transpose(1, 0, 2).reshape(rows, dim)
    y = pl.pallas_call(
        functools.partial(kernel, n_qa, sections),
        out_shape=jax.ShapeDtypeStruct((rows, dim), jnp.float32),
        in_specs=[
            pl.BlockSpec(memory_space=pltpu.VMEM),
            pl.BlockSpec(memory_space=pl.ANY),
            pl.BlockSpec(memory_space=pl.ANY),
        ],
        out_specs=pl.BlockSpec(memory_space=pltpu.VMEM),
        scratch_shapes=[
            pltpu.VMEM((2, rows // 2, dim), jnp.float32),
            pltpu.VMEM((2, rows // 2, dim), jnp.float32),
            pltpu.VMEM((rows // 2, dim), jnp.float32),
            pltpu.VMEM((2, rows // 2, dim), jnp.float32),
            pltpu.VMEM((rows // 2, 2 * dim), jnp.float32),
            pltpu.VMEM(gate_terms.shape, jnp.float32),
            pltpu.SMEM(path_bits.shape, jnp.int32),
            pltpu.VMEM((count, 4 * dim, 2 * dim), jnp.bfloat16),
            pltpu.VMEM((2, 2 * dim, 3 * dim), jnp.bfloat16),
            pltpu.SemaphoreType.DMA((2, n_qa)),
            pltpu.SemaphoreType.DMA((2, n_qa)),
            pltpu.SemaphoreType.DMA((2, 2, n_qa)),
            pltpu.SemaphoreType.DMA((2, 2, n_qa)),
            pltpu.SemaphoreType.DMA((2,)),
            pltpu.SemaphoreType.DMA((2, 2)),
        ],
        compiler_params=pltpu.CompilerParams(
            collective_id=0, has_side_effects=True, vmem_limit_bytes=48 * 2**20
        ),
    )(x, gate_terms, path_bits)
    return y.reshape(rows // 2, 2, dim).transpose(1, 0, 2).reshape(2, amps)


def solution(mesh):
    return jax.shard_map(
        per_device,
        mesh=mesh,
        in_specs=(P(None, ("paths", "qa", "qb")), P(), P("paths")),
        out_specs=P(None, ("paths", "qa", "qb")),
        check_vma=False,
    )
```

time: 61 us -> 58.3 us (0.956)
  Pallas kernels: 57.9 us -> 54.9 us
    pallas_call x1, Pallas kernels: 57.9 us -> 54.9 us  [per_device(): pl.pallas_call(functools.partial(kernel, n_qa, sections), out_shape=jax.S...]
where the time goes in v1:
time: 58.3 us; the launch traced here: 57.7 us
  Pallas kernels  54.9 us (94%)
  local copies, waits for them, and re-layouts  2.85 us (5%)
    pallas_call x1, Pallas kernels, per_device(): pl.pallas_call(functools.partial(kernel, n_qa, sections), out_shape=jax.S...  54.9 us
    unnamed x5, local copies, waits for them, and re-layouts  2.85 us

profile of v1, /device:TPU:29, one launch (start us, length us, event | category | flops | bytes accessed | tf_op | source)
XLA Modules:
  0.0 57.7 jit_solution(9122892534570587758)
XLA Ops:
  0.0 0.0 copy-start
  0.0 1.2 %copy-done = f32[2,131072]{1,0:T(2,128)S(1)} copy-done((f32[2,131072]{1,0:T(2,128)S(1)}, f32[2,131072]{1,0:T(2,128)}, u32[]{:S(2)}) %copy-start) | copy-done | bytes 1048600
  1.2 0.0 copy-start.1
  1.2 0.7 %copy-done.1 = s32[18]{0:T(128)S(1)} copy-done((s32[18]{0:T(128)S(1)}, s32[18]{0:T(128)}, u32[]{:S(2)}) %copy-start.1) | copy-done | bytes 96
  1.9 54.9 %shard_map.37 = f32[2048,128]{1,0:T(8,128)S(1)} custom-call(f32[2048,128]{1,0:T(8,128)S(1)} %bitcast.11, f32[18,2,2,128,128]{4,3,2,1,0:T(8,128)} %terms_hbm.1, s32[18]{0:T(128)S(1)} %copy-done.1), custom_call_target="tpu_custom_call" | custom-call | tf_op jit(solution)/shard_map/pallas_call | solution.py:245
  56.8 1.0 %copy.7 = f32[2,131072]{1,0:T(2,128)} copy(f32[2,131072]{1,0:T(2,128)S(1)} %bitcast.10) | data formatting | bytes 2097152
Async XLA Ops:
  0.0 1.2 %copy-start = (f32[2,131072]{1,0:T(2,128)S(1)}, f32[2,131072]{1,0:T(2,128)}, u32[]{:S(2)}) copy-start(f32[2,131072]{1,0:T(2,128)} %param.3) | copy-start | bytes 3145732
  1.2 0.7 %copy-start.1 = (s32[18]{0:T(128)S(1)}, s32[18]{0:T(128)}, u32[]{:S(2)}) copy-start(s32[18]{0:T(128)} %bits_hbm.1) | copy-start | bytes 220
